TPU v7x, 256 devices: a whole 4x4x8 slice. The times are simulated.
256 devices in a mesh: ep: 64 (over z, y, core), sp: 4 (over x).
Axes of the slice: x: 4, y: 4, z: 8, core: 2. Of those that a mesh axis runs over, the one named last changes fastest.
Arguments:
- stream: bfloat16 [32768, 4096], P(('ep', 'sp')), may hold values from -30 to 30
- query_base: bfloat16 [32768, 4096], P(('ep', 'sp')), may hold values from -40 to 40
- key_heads: bfloat16 [32768, 1024], P(('ep', 'sp')), may hold values from -6 to 6
- value_heads: bfloat16 [32768, 1024], P(('ep', 'sp')), may hold values from -12 to 12
- attention_gain: bfloat16 [4096], replicated, may hold values from 0.099609375 to 1.8984375
- expert_gain: bfloat16 [4096], replicated, may hold values from 0.099609375 to 1.8984375
- adapter_down: bfloat16 [4096, 128], P('sp'), may hold values from -0.09375 to 0.09375
- adapter_up: bfloat16 [4096, 128], P('sp'), may hold values from -1 to 1
- user_index: int32 [64], P('ep'), may hold values from 0 to 3
- routes: int32 [32768, 2], P('ep'), may hold values from 0 to 63, all different within a row; in each aligned block of 128 rows (0 to 127, 128 to 255, ...) at most 5 rows name the same one
- route_weights: int32 [32768, 2], P(('ep', 'sp')), may hold values from 1 to 4
- gate_weight: bfloat16 [64, 4096, 1536], P('ep', None, 'sp'), may hold values from -0.09375 to 0.09375
- up_weight: bfloat16 [64, 4096, 1536], P('ep', None, 'sp'), may hold values from -0.09375 to 0.09375
- down_weight: bfloat16 [64, 1536, 4096], P('ep', 'sp'), may hold values from -0.15625 to 0.15625
Outputs:
- hidden_state: bfloat16 [32768, 4096], P(('ep', 'sp'))
- moe_out: bfloat16 [32768, 4096], P(('ep', 'sp'))
Inputs may be any that keep to these rules, and one draw needn't show every extreme that they name: `routes`: each row names 2 different experts. In each aligned block of 128 rows (the tokens of one device) no expert is named more than 5 times, and in some block some expert is named exactly 5 times.
All inputs are finite; a program needn't handle non-finite values.
Results may differ from a plain program's by a relative error of at most 0.019.
Values may be sent and summed in bfloat16 or wider, within the bound.
No kernel may reach another device: no remote copies, remote signals or barrier semaphores. Data moves between devices by JAX's collectives and lax.ppermute only.
A program may use at most 128 MiB of HBM per device.

v0:
```python
import jax
import jax.numpy as jnp
from jax import lax
from jax.sharding import PartitionSpec as P

D = 4096
HEADS = 32
KV_HEADS = 8
HEAD = 128
RANK = 32
epsilon = 1e-06


def rms_scale(inputs, gain_vec):
    widened = inputs.astype(jnp.float32)
    return (
        widened
        * lax.rsqrt(jnp.mean(widened * widened, axis=-1, keepdims=True) + epsilon)
        * gain_vec.astype(jnp.float32)
    )


def route_slots(block_routes, experts):
    flat_routes = block_routes.reshape(-1)
    matches = (flat_routes[:, None] == jnp.arange(experts, dtype=jnp.int32)[None, :]).astype(
        jnp.int32
    )
    earlier = jnp.cumsum(matches, axis=0) - matches
    return (flat_routes, jnp.sum(earlier * matches, axis=1))


def attention_block(
    stream_rows, base_rows, key_rows, value_rows, user_id, attention_gain, adapter_down, adapter_up
):
    normed = rms_scale(stream_rows, attention_gain).astype(jnp.bfloat16)
    down_cols = lax.dynamic_slice_in_dim(adapter_down, user_id * RANK, RANK, 1)
    up_cols = lax.dynamic_slice_in_dim(adapter_up, user_id * RANK, RANK, 1)
    low_rank = jnp.dot(normed, down_cols, preferred_element_type=jnp.float32).astype(jnp.bfloat16)
    adapter_delta = jnp.dot(low_rank, up_cols.T, preferred_element_type=jnp.float32)
    queries = (base_rows.astype(jnp.float32) + adapter_delta).astype(jnp.bfloat16)
    group_size = HEADS // KV_HEADS
    row_total = queries.shape[0]
    query_heads = queries.reshape(row_total, KV_HEADS, group_size, HEAD)
    key_split = key_rows.reshape(-1, KV_HEADS, HEAD)
    value_split = value_rows.reshape(-1, KV_HEADS, HEAD)
    scores = jnp.einsum(
        "qhgd,khd->hgqk", query_heads, key_split, preferred_element_type=jnp.float32
    ) * HEAD ** (-0.5)
    row_max = jnp.max(scores, axis=-1, keepdims=True)
    exponent = jnp.exp(scores - row_max)
    attn_probs = (exponent / jnp.sum(exponent, axis=-1, keepdims=True)).astype(jnp.bfloat16)
    attended = jnp.einsum(
        "hgqk,khd->qhgd", attn_probs, value_split, preferred_element_type=jnp.float32
    ).reshape(row_total, D)
    return (stream_rows.astype(jnp.float32) + attended).astype(jnp.bfloat16)


def on_device(
    stream,
    query_base,
    key_heads,
    value_heads,
    attention_gain,
    expert_gain,
    adapter_down,
    adapter_up,
    user_index,
    routes,
    route_weights,
    gate_weight,
    up_weight,
    down_weight,
):
    key_all, value_all, down_all, up_all = (
        lax.all_gather(key_heads, "sp", axis=0, tiled=True),
        lax.all_gather(value_heads, "sp", axis=0, tiled=True),
        lax.all_gather(adapter_down, "sp", axis=0, tiled=True),
        lax.all_gather(adapter_up, "sp", axis=0, tiled=True),
    )
    hidden_state = attention_block(
        stream, query_base, key_all, value_all, user_index[0], attention_gain, down_all, up_all
    )
    normed_moe = rms_scale(hidden_state, expert_gain).astype(jnp.bfloat16)
    tokens_dev = stream.shape[0]
    top_count = routes.shape[1]
    model_width = stream.shape[1]
    experts = lax.axis_size("ep")
    capacity = max(2, (5 * tokens_dev * top_count + 4 * experts - 1) // (4 * experts))
    own_routes = lax.dynamic_slice_in_dim(routes, lax.axis_index("sp") * tokens_dev, tokens_dev, 0)
    flat_routes, slot_index = route_slots(own_routes, experts)
    position = flat_routes * capacity + slot_index
    padded = jnp.concatenate([normed_moe, jnp.zeros((1, model_width), jnp.bfloat16)], axis=0)
    token_ids = jnp.arange(tokens_dev * top_count, dtype=jnp.int32) // top_count
    slot_table = jnp.full((experts * capacity,), tokens_dev, jnp.int32).at[position].set(token_ids)
    outgoing = padded[slot_table].reshape(experts, capacity, model_width)
    received = lax.all_to_all(outgoing, "ep", split_axis=0, concat_axis=0, tiled=True)
    arrived = lax.all_gather(received, "sp", axis=0, tiled=True)
    all_rows = arrived.reshape(-1, model_width)
    gate_local = gate_weight[0]
    up_local = up_weight[0]
    down_local = down_weight[0]
    gate_out = jnp.dot(all_rows, gate_local, preferred_element_type=jnp.float32)
    up_out = jnp.dot(all_rows, up_local, preferred_element_type=jnp.float32)
    activated = (jax.nn.silu(gate_out) * up_out).astype(jnp.bfloat16)
    summed = lax.psum_scatter(
        jnp.dot(activated, down_local, preferred_element_type=jnp.float32).astype(jnp.bfloat16),
        "sp",
        scatter_dimension=0,
        tiled=True,
    )
    expert_out = summed.reshape(experts, capacity, model_width)
    returned = lax.all_to_all(expert_out, "ep", split_axis=0, concat_axis=0, tiled=True)
    picked = returned.reshape(experts * capacity, model_width)[position].reshape(
        tokens_dev, top_count, model_width
    )
    route_share = route_weights.astype(jnp.float32)
    route_share = route_share / jnp.sum(route_share, axis=1, keepdims=True)
    moe_out = jnp.sum(picked.astype(jnp.float32) * route_share[:, :, None], axis=1).astype(
        jnp.bfloat16
    )
    return (hidden_state, moe_out)


def solution(mesh):
    in_specs = (
        P(("ep", "sp"), None),
        P(("ep", "sp"), None),
        P(("ep", "sp"), None),
        P(("ep", "sp"), None),
        P(),
        P(),
        P("sp", None),
        P("sp", None),
        P("ep"),
        P("ep", None),
        P(("ep", "sp"), None),
        P("ep", None, "sp"),
        P("ep", None, "sp"),
        P("ep", "sp", None),
    )
    out_specs = (P(("ep", "sp"), None), P(("ep", "sp"), None))
    return jax.shard_map(
        on_device, mesh=mesh, in_specs=in_specs, out_specs=out_specs, check_vma=False
    )
```

profile of v0, /device:TPU:8, one launch (start us, length us, event | category | flops | bytes accessed | tf_op | source)
XLA Modules:
  0.0 679.8 jit_solution(350134085212804269)
XLA Ops:
  7.2 0.7 all-gather.6.cloned.1.call-update
  8.0 0.7 all-gather.8.cloned.1.call-update
  8.7 1.8 copy.30
  10.6 0.5 all-gather.12.cloned.1.call-update
  11.2 0.7 broadcast_multiply_fusion
  11.9 0.1 copy.36
  12.0 0.1 eq.29
  12.1 0.1 eq.25
  12.9 0.6 reduce-window.6
  13.6 0.2 slice_reduce_fusion
  13.9 0.1 mul.109
  14.2 1.4 scatter_custom_fusion
  15.6 0.7 convert_element_type.61
  16.3 1.5 fusion.21
  17.8 21.4 %all-gather.6.cloned.1.call-done = bf16[4096,128]{1,0:T(8,128)(2,1)} async-done(((bf16[1024,128]{1,0:T(8,128)(2,1)}), bf16[4096,128]{1,0:T(8,128)(2,1)}) %all-gather.6.cloned.1.call-update) | async-done | bytes 1048592 | tf_op jit(solution)/shard_map/all_gather | solution.py:77
  39.2 28.7 %all-gather.8.cloned.1.call-done = bf16[4096,128]{1,0:T(8,128)(2,1)} async-done(((bf16[1024,128]{1,0:T(8,128)(2,1)}), bf16[4096,128]{1,0:T(8,128)(2,1)}) %all-gather.8.cloned.1.call-update) | async-done | bytes 1048592 | tf_op jit(solution)/shard_map/all_gather | solution.py:78
  67.9 4.9 fusion.6
  72.8 3.0 reshape.101
  75.8 22.7 %all-gather.10.cloned.1.call-done = bf16[512,1024]{0,1:T(8,128)(2,1)} async-done(((bf16[128,1024]{0,1:T(8,128)(2,1)}), bf16[512,1024]{0,1:T(8,128)(2,1)}) %all-gather.10.cloned.1.call-update) | async-done | bytes 1048592 | tf_op jit(solution)/shard_map/all_gather | solution.py:75
  98.5 2.8 fusion.32
  101.3 3.2 copy-done.1
  104.5 2.4 fusion.60
  107.0 20.8 %all-gather.12.cloned.1.call-done = bf16[512,1024]{1,0:T(8,128)(2,1)} async-done(((bf16[128,1024]{1,0:T(8,128)(2,1)}), bf16[512,1024]{1,0:T(8,128)(2,1)}) %all-gather.12.cloned.1.call-update) | async-done | bytes 1048592 | tf_op jit(solution)/shard_map/all_gather | solution.py:76
  127.7 2.3 copy.33
  130.0 12.1 %fusion.8 = f32[8,4,128,128]{2,3,1,0:T(8,128)} fusion(bf16[512,8,128,1]{0,2,3,1:T(8,128)(2,1)} %bitcast.73, f32[8,4,128]{2,1,0:T(4,128)S(1)} %fusion.60, f32[8,128,4,512]{3,1,2,0:T(8,128)} %copy-done.1), kind=kOutput, calls=%fused_computation.15 | convolution fusion | flops 547361280 | bytes 11550720 | tf_op jit(solution)/shard_map/hgqk,khd->qhgd/dot_general | solution.py:52
  142.2 2.9 copy.34
  145.1 2.3 fusion.18
  147.4 1.0 copy-done.2
  148.3 0.3 fusion.20
  148.7 1.1 concatenate.3
  149.8 9.5 %gather_fusion = bf16[320,4096]{1,0:T(8,128)(2,1)} fusion(bf16[129,4096]{1,0:T(8,128)(2,1)} %concatenate.3, s32[1024]{0:T(1024)S(1)} %pad_clamp_fusion.1), kind=kCustom, calls=%fused_computation | custom fusion | bytes 5244160 | tf_op jit(solution)/shard_map/gather | solution.py:95
  159.3 4.7 reshape.106
  164.0 106.9 %all_to_all.10 = bf16[64,5,4096]{2,1,0:T(8,128)(2,1)S(1)} all-to-all(bf16[64,5,4096]{2,1,0:T(8,128)(2,1)} %reshape.106), channel_id=1, replica_groups=mesh['ep'=64,'sp'=4] {'ep'}, dimensions={0} | all-to-all | bytes 5242880 | tf_op jit(solution)/shard_map/all_to_all | solution.py:96
  270.9 3.2 copy.39
  274.2 98.8 %all-gather.14.cloned.1.call-done = bf16[256,5,4096]{2,0,1:T(8,128)(2,1)} async-done(((bf16[64,5,4096]{2,0,1:T(8,128)(2,1)}), bf16[256,5,4096]{2,0,1:T(8,128)(2,1)}) %all-gather.14.cloned.1.call-update) | async-done | bytes 10485776 | tf_op jit(solution)/shard_map/all_gather | solution.py:97
  372.9 15.2 %copy.40 = bf16[256,5,4096]{2,1,0:T(8,128)(2,1)} copy(bf16[256,5,4096]{2,0,1:T(8,128)(2,1)} %all-gather.14.cloned.1.call-done) | data formatting | bytes 20971520 | tf_op jit(solution)/shard_map/all_gather | solution.py:97
  388.2 16.8 %reshape.107 = bf16[1280,4096]{1,0:T(8,128)(2,1)} reshape(bf16[256,5,4096]{2,1,0:T(8,128)(2,1)} %copy.40) | data formatting | bytes 20971520 | tf_op jit(solution)/shard_map/reshape | solution.py:98
  405.0 10.1 %fusion.11 = f32[1280,384]{1,0:T(8,128)} fusion(bf16[1280,4096]{1,0:T(8,128)(2,1)} %reshape.107, bf16[1,4096,384]{2,1,0:T(8,128)(2,1)} %param.25), kind=kOutput, calls=%fused_computation.19 | convolution fusion | flops 4026531840 | bytes 15597568 | tf_op jit(solution)/shard_map/dot_general | solution.py:102
  415.1 17.3 %convolution_convert_fusion = bf16[1280,4096]{1,0:T(8,128)(2,1)} fusion(bf16[1,384,4096]{2,1,0:T(8,128)(2,1)S(1)} %copy-done, bf16[1280,4096]{1,0:T(8,128)(2,1)} %reshape.107, bf16[1,4096,384]{2,1,0:T(8,128)(2,1)} %param.26, f32[1280,384]{1,0:T(8,128)} %fusion.11), kind=kOutput, calls=%fused_computation.4 | convolution fusion | flops 8061255680 | bytes 29229056 | tf_op jit(solution)/shard_map/dot_general | solution.py:106
  432.5 101.2 %reduce-scatter.2.cloned.1.call-done = bf16[320,4096]{1,0:T(8,128)(2,1)} async-done(((bf16[1280,4096]{1,0:T(8,128)(2,1)}), bf16[320,4096]{1,0:T(8,128)(2,1)}) %reduce-scatter.2.cloned.1.call-update) | async-done | bytes 2621456 | tf_op jit(solution)/shard_map/reduce_scatter | solution.py:105
  533.7 4.7 reshape.108
  538.4 11.3 %all-to-all-start.1 = ((bf16[64,5,4096]{2,1,0:T(8,128)(2,1)}), bf16[64,5,4096]{2,1,0:T(8,128)(2,1)}, u32[]{:S(2)}, u32[]{:S(2)}) async-start(bf16[64,5,4096]{2,1,0:T(8,128)(2,1)} %reshape.108), calls=%async_computation.2 | async-start | bytes 8388608 | tf_op jit(solution)/shard_map/all_to_all | solution.py:112
  549.7 0.1 copy.41
  549.8 95.8 %all-to-all-done.1 = bf16[64,5,4096]{2,1,0:T(8,128)(2,1)} async-done(((bf16[64,5,4096]{2,1,0:T(8,128)(2,1)}), bf16[64,5,4096]{2,1,0:T(8,128)(2,1)}, u32[]{:S(2)}, u32[]{:S(2)}) %all-to-all-start.1) | async-done | bytes 2621472 | tf_op jit(solution)/shard_map/all_to_all | solution.py:112
  645.6 4.8 reshape.109
  650.3 7.4 %gather_fusion.1 = bf16[256,4096]{1,0:T(8,128)(2,1)} fusion(bf16[320,4096]{1,0:T(8,128)(2,1)} %reshape.109, s32[1024]{0:T(1024)S(1)} %pad_clamp_fusion), kind=kCustom, calls=%fused_computation.1 | custom fusion | bytes 4195328 | tf_op jit(solution)/shard_map/gather | solution.py:113
  657.7 5.4 reshape.110
  663.1 9.6 %multiply_reduce_fusion = bf16[128,4096]{1,0:T(8,128)(2,1)} fusion(f32[128,2,4096]{2,1,0:T(2,128)} %reshape.110, f32[128,2]{1,0:T(8,128)S(1)} %copy.41), kind=kLoop, calls=%fused_computation.13 | loop fusion | flops 1572864 | bytes 5243904 | tf_op jit(solution)/shard_map/reduce_sum | solution.py:118
  (32 shorter events, 0.6 us)
Async XLA Ops:
  7.2 408.0 %copy-start = (bf16[1,384,4096]{2,1,0:T(8,128)(2,1)S(1)}, bf16[1,384,4096]{2,1,0:T(8,128)(2,1)}, u32[]{:S(2)}) copy-start(bf16[1,384,4096]{2,1,0:T(8,128)(2,1)} %param.27) | copy-start | bytes 9437188
  7.2 10.6 %copy-start.3 = (bf16[4096]{0:T(1024)(128)(2,1)S(1)}, bf16[4096]{0:T(1024)(128)(2,1)}, u32[]{:S(2)}) copy-start(bf16[4096]{0:T(1024)(128)(2,1)} %param.19) | copy-start | bytes 24580
  7.2 32.1 %all-gather.6.cloned.1.call-start = ((), (), s32[]{:S(2)}) async-start(), calls=%async_computation.3 | async-start | bytes 1310720 | tf_op jit(solution)/shard_map/all_gather | solution.py:77
  7.9 60.0 %all-gather.8.cloned.1.call-start = ((), (), s32[]{:S(2)}) async-start(), calls=%async_computation.4 | async-start | bytes 1310720 | tf_op jit(solution)/shard_map/all_gather | solution.py:78
  8.7 89.9 %all-gather.10.cloned.1.call-start = ((), (), s32[]{:S(2)}) async-start(), calls=%async_computation.5 | async-start | bytes 1310720 | tf_op jit(solution)/shard_map/all_gather | solution.py:75
  10.6 117.2 %all-gather.12.cloned.1.call-start = ((), (), s32[]{:S(2)}) async-start(), calls=%async_computation.6 | async-start | bytes 1310720 | tf_op jit(solution)/shard_map/all_gather | solution.py:76
  11.1 361.8 %all-gather.14.cloned.1.call-start = ((), (), s32[]{:S(2)}) async-start(), calls=%async_computation.7 | async-start | bytes 13107200 | tf_op jit(solution)/shard_map/all_gather | solution.py:97
  101.3 3.2 copy-start.1
  147.3 1.0 copy-start.2
  274.1 259.5 %reduce-scatter.2.cloned.1.call-start = ((), (), s32[]{:S(2)}) async-start(), calls=%async_computation.8 | async-start | bytes 13107200 | tf_op jit(solution)/shard_map/reduce_scatter | solution.py:105
  538.3 11.3 %copy-start.4 = (s32[128,2]{0,1:T(2,128)S(1)}, s32[128,2]{0,1:T(2,128)}, u32[]{:S(2)}) copy-start(s32[128,2]{0,1:T(2,128)} %param.24) | copy-start | bytes 3076
  538.4 107.2 %all-to-all-start.1 = ((bf16[64,5,4096]{2,1,0:T(8,128)(2,1)}), bf16[64,5,4096]{2,1,0:T(8,128)(2,1)}, u32[]{:S(2)}, u32[]{:S(2)}) async-start(bf16[64,5,4096]{2,1,0:T(8,128)(2,1)} %reshape.108), calls=%async_computation.2 | async-start | bytes 8388608 | tf_op jit(solution)/shard_map/all_to_all | solution.py:112
Sparse Core Ops, SparseCore 0:
  9.8 29.3 all-gather.5
  41.0 26.8 all-gather.7
  69.7 28.7 all-gather.9
  100.2 27.5 all-gather.11
  274.2 98.6 all-gather.13
  432.6 101.0 reduce-scatter.1
where the time goes:
time: 685 us; the launch traced here: 680 us
  waiting for transfers between devices  391 us (57%)
  blocking collectives  107 us (16%)
  local copies, waits for them, and re-layouts  89.4 us (13%)
  matrix products  47.2 us (7%)
  other arithmetic  18.4 us (3%)
  between operations  15.2 us (2%)
  starting transfers between devices  11.5 us (2%)
    all_to_all x1, blocking collectives, on_device(): lax.all_to_all(outgoing, 'ep', split_axis=0, concat_axis=0, tiled=True)  107 us
    reduce_scatter x1, waiting for transfers between devices, on_device(): lax.psum_scatter(jnp.dot(activated, down_local, preferred_element_type=jn...  101 us
    all_gather x1, waiting for transfers between devices, on_device(): arrived = lax.all_gather(received, 'sp', axis=0, tiled=True)  98.8 us
    all_to_all x1, waiting for transfers between devices, on_device(): lax.all_to_all(expert_out, 'ep', split_axis=0, concat_axis=0, tiled=True)  95.8 us
    all_gather x1, waiting for transfers between devices, on_device(): lax.all_gather(adapter_up, 'sp', axis=0, tiled=True)  28.7 us
    all_gather x1, waiting for transfers between devices, on_device(): lax.all_gather(key_heads, 'sp', axis=0, tiled=True)  22.7 us
    all_gather x1, waiting for transfers between devices, on_device(): lax.all_gather(adapter_down, 'sp', axis=0, tiled=True)  21.4 us
    all_gather x1, waiting for transfers between devices, on_device(): lax.all_gather(value_heads, 'sp', axis=0, tiled=True)  20.8 us
  transfers between devices with their start and end apart: 7, of which 7 were waited for; matrix products, arithmetic and copies ran while one was open for 3% of the time, Pallas kernels for 0%

commit v1 on v0

--- a/solution.py
+++ b/solution.py
@@ -9,6 +9,18 @@
 HEAD = 128
 RANK = 32
 epsilon = 1e-06
+
+
+def _deliver_classes(obj, axis_key):
+    return jnp.concatenate(
+        lax.all_to_all(
+            jnp.stack(lax.axis_size(axis_key) * [obj], axis=0),
+            axis_name=axis_key,
+            split_axis=0,
+            concat_axis=0,
+        ),
+        axis=0,
+    )
 
 
 def rms_scale(inputs, gain_vec):
@@ -73,7 +85,7 @@
 ):
     key_all, value_all, down_all, up_all = (
         lax.all_gather(key_heads, "sp", axis=0, tiled=True),
-        lax.all_gather(value_heads, "sp", axis=0, tiled=True),
+        _deliver_classes(value_heads, axis_key="sp"),
         lax.all_gather(adapter_down, "sp", axis=0, tiled=True),
         lax.all_gather(adapter_up, "sp", axis=0, tiled=True),
     )

time: 685 us -> 664 us (0.969)
  waiting for transfers between devices: 391 us -> 363 us
    all_gather x1 -> x0, waiting for transfers between devices: 20.8 us -> none  [on_device(): lax.all_gather(value_heads, 'sp', axis=0, tiled=True)]
    all_gather x1, waiting for transfers between devices: 21.4 us -> 1.99 us  [on_device(): lax.all_gather(adapter_down, 'sp', axis=0, tiled=True)]
    all_to_all x0 -> x1, waiting for transfers between devices: none -> 9.91 us  [_deliver_classes(): lax.all_to_all(jnp.stack(lax.axis_size(axis_key) * [obj], axis=0), axis_n...]
where the time goes in v1:
time: 664 us; the launch traced here: 660 us
  waiting for transfers between devices  363 us (55%)
  blocking collectives  107 us (16%)
  local copies, waits for them, and re-layouts  95.1 us (14%)
  matrix products  47.2 us (7%)
  other arithmetic  17.7 us (3%)
  starting transfers between devices  15.7 us (2%)
  between operations  14.9 us (2%)
    all_to_all x1, blocking collectives, on_device(): lax.all_to_all(outgoing, 'ep', split_axis=0, concat_axis=0, tiled=True)  107 us
    reduce_scatter x1, waiting for transfers between devices, on_device(): lax.psum_scatter(jnp.dot(activated, down_local, preferred_element_type=jn...  101 us
    all_gather x1, waiting for transfers between devices, on_device(): arrived = lax.all_gather(received, 'sp', axis=0, tiled=True)  99.4 us
    all_to_all x1, waiting for transfers between devices, on_device(): lax.all_to_all(expert_out, 'ep', split_axis=0, concat_axis=0, tiled=True)  95.8 us
    all_gather x1, waiting for transfers between devices, on_device(): lax.all_gather(adapter_up, 'sp', axis=0, tiled=True)  29.8 us
    all_gather x1, waiting for transfers between devices, on_device(): lax.all_gather(key_heads, 'sp', axis=0, tiled=True)  23.1 us
    dot_general x1, matrix products, on_device(): jnp.dot(activated, down_local, preferred_element_type=jnp.float32)  17.3 us
    reshape x1, local copies, waits for them, and re-layouts, on_device(): all_rows = arrived.reshape(-1, model_width)  16.8 us
  transfers between devices with their start and end apart: 7, of which 7 were waited for; matrix products, arithmetic and copies ran while one was open for 3% of the time, Pallas kernels for 0%

profile of v1, /device:TPU:8, one launch (start us, length us, event | category | flops | bytes accessed | tf_op | source)
XLA Modules:
  0.0 660.0 jit_solution(14969424267927148718)
XLA Ops:
  7.2 0.7 all-gather.5.cloned.1.call-update
  8.0 0.7 all-gather.7.cloned.1.call-update
  8.7 1.1 copy.33
  9.8 1.1 stack.2
  10.9 4.3 all-to-all-start
  15.2 1.8 copy.30
  17.1 0.7 broadcast_multiply_fusion
  17.9 0.1 eq.29
  18.0 0.1 eq.25
  18.2 0.6 reduce-window.6
  18.8 0.2 slice_reduce_fusion
  19.2 0.1 mul.109
  20.1 1.7 scatter_custom_fusion
  21.8 1.5 fusion.21
  23.4 9.9 %all-to-all-done = bf16[4,128,1024]{1,2,0:T(8,128)(2,1)} async-done(((bf16[4,128,1024]{1,2,0:T(8,128)(2,1)}), bf16[4,128,1024]{1,2,0:T(8,128)(2,1)}, u32[]{:S(2)}, u32[]{:S(2)}) %all-to-all-start) | async-done | bytes 1048608 | tf_op jit(solution)/shard_map/all_to_all | solution.py:16
  33.3 3.0 copy.34
  36.3 2.3 reshape.135
  38.5 2.0 all-gather.5.cloned.1.call-done
  40.5 29.8 %all-gather.7.cloned.1.call-done = bf16[4096,128]{1,0:T(8,128)(2,1)} async-done(((bf16[1024,128]{1,0:T(8,128)(2,1)}), bf16[4096,128]{1,0:T(8,128)(2,1)}) %all-gather.7.cloned.1.call-update) | async-done | bytes 1048592 | tf_op jit(solution)/shard_map/all_gather | solution.py:90
  70.4 4.9 fusion.6
  75.2 2.6 reshape.100
  77.8 23.1 %all-gather.9.cloned.1.call-done = bf16[512,1024]{0,1:T(8,128)(2,1)} async-done(((bf16[128,1024]{0,1:T(8,128)(2,1)}), bf16[512,1024]{0,1:T(8,128)(2,1)}) %all-gather.9.cloned.1.call-update) | async-done | bytes 1048592 | tf_op jit(solution)/shard_map/all_gather | solution.py:87
  100.9 2.8 fusion.33
  103.7 3.2 copy-done.1
  106.9 2.4 fusion.61
  109.4 12.1 %fusion.8 = f32[8,4,128,128]{2,3,1,0:T(8,128)} fusion(f32[8,4,128]{2,1,0:T(4,128)S(1)} %fusion.61, bf16[512,8,128,1]{0,2,1,3:T(8,128)(2,1)} %reshape.135, f32[8,128,4,512]{3,1,2,0:T(8,128)} %copy-done.1), kind=kOutput, calls=%fused_computation.15 | convolution fusion | flops 547361280 | bytes 11550720 | tf_op jit(solution)/shard_map/hgqk,khd->qhgd/dot_general | solution.py:64
  121.5 2.9 copy.35
  124.4 2.3 fusion.18
  126.7 1.0 copy-done.2
  127.7 0.3 fusion.20
  128.0 1.1 concatenate.3
  129.2 10.0 %gather_fusion = bf16[320,4096]{1,0:T(8,128)(2,1)} fusion(bf16[129,4096]{1,0:T(8,128)(2,1)} %concatenate.3, s32[1024]{0:T(1024)S(1)} %pad_clamp_fusion.1), kind=kCustom, calls=%fused_computation | custom fusion | bytes 5244160 | tf_op jit(solution)/shard_map/gather | solution.py:107
  139.1 4.7 reshape.104
  143.9 106.8 %all_to_all.15 = bf16[64,5,4096]{2,1,0:T(8,128)(2,1)S(1)} all-to-all(bf16[64,5,4096]{2,1,0:T(8,128)(2,1)} %reshape.104), channel_id=1, replica_groups=mesh['ep'=64,'sp'=4] {'ep'}, dimensions={0} | all-to-all | bytes 5242880 | tf_op jit(solution)/shard_map/all_to_all | solution.py:108
  250.6 3.2 copy.40
  253.9 99.4 %all-gather.11.cloned.1.call-done = bf16[256,5,4096]{2,0,1:T(8,128)(2,1)} async-done(((bf16[64,5,4096]{2,0,1:T(8,128)(2,1)}), bf16[256,5,4096]{2,0,1:T(8,128)(2,1)}) %all-gather.11.cloned.1.call-update) | async-done | bytes 10485776 | tf_op jit(solution)/shard_map/all_gather | solution.py:109
  353.3 15.4 %copy.41 = bf16[256,5,4096]{2,1,0:T(8,128)(2,1)} copy(bf16[256,5,4096]{2,0,1:T(8,128)(2,1)} %all-gather.11.cloned.1.call-done) | data formatting | bytes 20971520 | tf_op jit(solution)/shard_map/all_gather | solution.py:109
  368.7 16.8 %reshape.105 = bf16[1280,4096]{1,0:T(8,128)(2,1)} reshape(bf16[256,5,4096]{2,1,0:T(8,128)(2,1)} %copy.41) | data formatting | bytes 20971520 | tf_op jit(solution)/shard_map/reshape | solution.py:110
  385.5 10.1 %fusion.11 = f32[1280,384]{1,0:T(8,128)} fusion(bf16[1280,4096]{1,0:T(8,128)(2,1)} %reshape.105, bf16[1,4096,384]{2,1,0:T(8,128)(2,1)} %param.25), kind=kOutput, calls=%fused_computation.19 | convolution fusion | flops 4026531840 | bytes 15597568 | tf_op jit(solution)/shard_map/dot_general | solution.py:114
  395.7 17.3 %convolution_convert_fusion = bf16[1280,4096]{1,0:T(8,128)(2,1)} fusion(bf16[1,384,4096]{2,1,0:T(8,128)(2,1)S(1)} %copy-done, bf16[1280,4096]{1,0:T(8,128)(2,1)} %reshape.105, bf16[1,4096,384]{2,1,0:T(8,128)(2,1)} %param.26, f32[1280,384]{1,0:T(8,128)} %fusion.11), kind=kOutput, calls=%fused_computation.4 | convolution fusion | flops 8061255680 | bytes 29229056 | tf_op jit(solution)/shard_map/dot_general | solution.py:118
  413.0 101.2 %reduce-scatter.2.cloned.1.call-done = bf16[320,4096]{1,0:T(8,128)(2,1)} async-done(((bf16[1280,4096]{1,0:T(8,128)(2,1)}), bf16[320,4096]{1,0:T(8,128)(2,1)}) %reduce-scatter.2.cloned.1.call-update) | async-done | bytes 2621456 | tf_op jit(solution)/shard_map/reduce_scatter | solution.py:117
  514.2 4.7 reshape.106
  518.9 11.3 %all-to-all-start.2 = ((bf16[64,5,4096]{2,1,0:T(8,128)(2,1)}), bf16[64,5,4096]{2,1,0:T(8,128)(2,1)}, u32[]{:S(2)}, u32[]{:S(2)}) async-start(bf16[64,5,4096]{2,1,0:T(8,128)(2,1)} %reshape.106), calls=%async_computation.3 | async-start | bytes 8388608 | tf_op jit(solution)/shard_map/all_to_all | solution.py:124
  530.3 95.8 %all-to-all-done.2 = bf16[64,5,4096]{2,1,0:T(8,128)(2,1)} async-done(((bf16[64,5,4096]{2,1,0:T(8,128)(2,1)}), bf16[64,5,4096]{2,1,0:T(8,128)(2,1)}, u32[]{:S(2)}, u32[]{:S(2)}) %all-to-all-start.2) | async-done | bytes 2621472 | tf_op jit(solution)/shard_map/all_to_all | solution.py:124
  626.1 4.8 reshape.107
  630.9 7.4 %gather_fusion.1 = bf16[256,4096]{1,0:T(8,128)(2,1)} fusion(bf16[320,4096]{1,0:T(8,128)(2,1)} %reshape.107, s32[1024]{0:T(1024)S(1)} %pad_clamp_fusion), kind=kCustom, calls=%fused_computation.1 | custom fusion | bytes 4195328 | tf_op jit(solution)/shard_map/gather | solution.py:125
  638.2 5.4 reshape.108
  643.7 9.6 %multiply_reduce_fusion = bf16[128,4096]{1,0:T(8,128)(2,1)} fusion(f32[128,2,4096]{2,1,0:T(2,128)} %reshape.108, f32[128,2]{1,0:T(8,128)S(1)} %copy.42), kind=kLoop, calls=%fused_computation.13 | loop fusion | flops 1572864 | bytes 5243904 | tf_op jit(solution)/shard_map/reduce_sum | solution.py:130
  (36 shorter events, 0.8 us)
Async XLA Ops:
  7.2 388.5 %copy-start = (bf16[1,384,4096]{2,1,0:T(8,128)(2,1)S(1)}, bf16[1,384,4096]{2,1,0:T(8,128)(2,1)}, u32[]{:S(2)}) copy-start(bf16[1,384,4096]{2,1,0:T(8,128)(2,1)} %param.27) | copy-start | bytes 9437188
  7.2 12.9 %copy-start.3 = (bf16[4096]{0:T(1024)(128)(2,1)S(1)}, bf16[4096]{0:T(1024)(128)(2,1)}, u32[]{:S(2)}) copy-start(bf16[4096]{0:T(1024)(128)(2,1)} %param.18) | copy-start | bytes 24580
  7.2 12.9 %copy-start.4 = (bf16[4096]{0:T(1024)(128)(2,1)S(1)}, bf16[4096]{0:T(1024)(128)(2,1)}, u32[]{:S(2)}) copy-start(bf16[4096]{0:T(1024)(128)(2,1)} %param.19) | copy-start | bytes 24580
  7.2 33.3 %all-gather.5.cloned.1.call-start = ((), (), s32[]{:S(2)}) async-start(), calls=%async_computation.4 | async-start | bytes 1310720 | tf_op jit(solution)/shard_map/all_gather | solution.py:89
  7.9 62.4 %all-gather.7.cloned.1.call-start = ((), (), s32[]{:S(2)}) async-start(), calls=%async_computation.5 | async-start | bytes 1310720 | tf_op jit(solution)/shard_map/all_gather | solution.py:90
  10.9 22.4 %all-to-all-start = ((bf16[4,128,1024]{1,2,0:T(8,128)(2,1)}), bf16[4,128,1024]{1,2,0:T(8,128)(2,1)}, u32[]{:S(2)}, u32[]{:S(2)}) async-start(bf16[4,128,1024]{1,2,0:T(8,128)(2,1)} %stack.2), calls=%async_computation | async-start | bytes 2097152 | tf_op jit(solution)/shard_map/all_to_all | solution.py:16
  15.2 85.7 %all-gather.9.cloned.1.call-start = ((), (), s32[]{:S(2)}) async-start(), calls=%async_computation.6 | async-start | bytes 1310720 | tf_op jit(solution)/shard_map/all_gather | solution.py:87
  17.0 336.3 %all-gather.11.cloned.1.call-start = ((), (), s32[]{:S(2)}) async-start(), calls=%async_computation.7 | async-start | bytes 13107200 | tf_op jit(solution)/shard_map/all_gather | solution.py:109
  103.7 3.2 copy-start.1
  126.7 1.0 copy-start.2
  253.9 260.3 %reduce-scatter.2.cloned.1.call-start = ((), (), s32[]{:S(2)}) async-start(), calls=%async_computation.8 | async-start | bytes 13107200 | tf_op jit(solution)/shard_map/reduce_scatter | solution.py:117
  518.9 11.3 %copy-start.5 = (s32[128,2]{0,1:T(2,128)S(1)}, s32[128,2]{0,1:T(2,128)}, u32[]{:S(2)}) copy-start(s32[128,2]{0,1:T(2,128)} %param.24) | copy-start | bytes 3076
  518.9 107.2 %all-to-all-start.2 = ((bf16[64,5,4096]{2,1,0:T(8,128)(2,1)}), bf16[64,5,4096]{2,1,0:T(8,128)(2,1)}, u32[]{:S(2)}, u32[]{:S(2)}) async-start(bf16[64,5,4096]{2,1,0:T(8,128)(2,1)} %reshape.106), calls=%async_computation.3 | async-start | bytes 8388608 | tf_op jit(solution)/shard_map/all_to_all | solution.py:124
Sparse Core Ops, SparseCore 0:
  9.8 30.6 all-gather.4
  42.3 27.9 all-gather.6
  72.2 28.7 all-gather.8
  254.0 99.2 all-gather.10
  413.1 101.0 reduce-scatter.1
